TPU v7x, 256 devices: a whole 4x4x8 slice. The times are simulated.
256 devices in a mesh: dp: 32 (over z, y_lo, core), grp: 8 (over y_hi, x).
Axes of the slice: x: 4, y: 4 (y_hi: 2, y_lo: 2; y = y_hi * 2 + y_lo), z: 8, core: 2. Of those that a mesh axis runs over, the one named last changes fastest.
Arguments:
- activations: bfloat16 [16384, 3072], P('dp', 'grp'), may hold values from -125 to 125
- cotangents: bfloat16 [16384, 3072], P('dp', 'grp'), may hold values from -125 to 125
Outputs:
- update: float32 [3072, 3072], P('dp', 'grp')
All inputs are finite; a program needn't handle non-finite values.
Results may differ from a plain program's by a relative error of at most 0.009.
Values may be sent and summed in bfloat16 or wider, within the bound.
No kernel may reach another device: no remote copies, remote signals or barrier semaphores. Data moves between devices by JAX's collectives and lax.ppermute only.
A program may use at most 128 MiB of HBM per device.

v0:
```python
import jax
import jax.numpy as jnp
from jax import lax
from jax.sharding import Mesh
from jax.sharding import PartitionSpec as P

D = 3072
ITERS = 3
GRP = ("grp_0", "grp_1")
DP = ("dp_0", "dp_1", "dp_2")
DP_GRP = ("dp_0", "dp_1", "dp_2", "grp_0", "grp_1")
damping = 0.05
epsilon = 1e-06


def copy_for_each(shard, axis):
    copies = jnp.broadcast_to(shard, (lax.axis_size(axis), *shard.shape))
    return lax.all_to_all(copies, axis, split_axis=0, concat_axis=0, tiled=True)


def in_order(tiles, dim):
    lengths = list(tiles.shape[1:])
    lengths[dim] *= tiles.shape[0]
    return jnp.moveaxis(tiles, 0, dim).reshape(lengths)


def gather_directly(shard, axis, dim):
    tiles = copy_for_each(shard, axis)
    return in_order(tiles, dim)


def sent_together(arrays, axis, dim, along):
    both = jnp.concatenate(arrays, axis=along)
    whole, at, outs = (lax.all_gather(both, axis, axis=dim, tiled=True), 0, [])
    for a in arrays:
        outs.append(lax.slice_in_dim(whole, at, at + a.shape[along], axis=along))
        at += a.shape[along]
    return tuple(outs)


def own_block(tiles, axes, turns):
    inside = tiles.shape[1:]
    tiles = tiles.reshape(*(lax.axis_size(a) for a in axes), *inside)
    tiles = jnp.moveaxis(tiles, turns, range(len(axes))).reshape(-1, *inside)
    for k in turns:
        tiles = lax.psum_scatter(tiles, axes[k], scatter_dimension=0, tiled=True)
    return tiles[0]


def split_up(shard, dim, count):
    before, after = (shard.shape[:dim], shard.shape[dim + 1 :])
    return jnp.moveaxis(shard.reshape(*before, count, -1, *after), dim, 0)


def summed_rows(shard, axes, turns, dim):
    count = lax.axis_size(axes)
    return own_block(split_up(shard, dim, count), axes, turns)


def over_axes(shard, axes):
    for axis in axes:
        shard = lax.psum(shard, axis)
    return shard


def row_panel(stacked_tiles):
    return gather_directly(stacked_tiles, GRP, 2)


def times_columns(panel_rows, stacked_tiles):
    return jnp.einsum(
        "fri,fic->frc",
        panel_rows,
        lax.all_gather(stacked_tiles, DP, axis=1, tiled=True),
        preferred_element_type=jnp.float32,
    )


def shards(activations, cotangents):
    dp_count = lax.axis_size(DP)
    grp_count = lax.axis_size(GRP)
    tile_rows = D // dp_count
    tile_cols = D // grp_count
    dp_index = lax.axis_index(DP)
    grp_index = lax.axis_index(GRP)
    whole_inputs, whole_grads = sent_together((activations, cotangents), GRP, 1, 0)
    contract = (((0,), (0,)), ((), ()))
    row_ids = dp_index * tile_rows + lax.iota(jnp.int32, tile_rows)[:, None]
    col_ids = grp_index * tile_cols + lax.iota(jnp.int32, tile_cols)[None, :]
    diag_tile = (row_ids == col_ids).astype(jnp.float32)
    diag_rows = (row_ids == lax.iota(jnp.int32, D)[None, :]).astype(jnp.float32)
    gradient_tile = None
    grads_part = whole_grads
    input_cov = lax.dot_general(
        whole_inputs, activations, contract, preferred_element_type=jnp.float32
    )
    grad_cov = lax.dot_general(grads_part, cotangents, contract, preferred_element_type=jnp.float32)
    input_cov, grad_cov = (input_cov, grad_cov)
    grads_part = whole_grads
    weight_grad = lax.dot_general(
        grads_part, activations, contract, preferred_element_type=jnp.float32
    )
    sum_tiles = summed_rows(
        jnp.concatenate([input_cov, grad_cov, weight_grad], axis=1), DP, (2, 0, 1), 0
    )
    gradient_tile = sum_tiles[:, 2 * tile_cols :]
    factor_tiles = jnp.stack([sum_tiles[:, :tile_cols], sum_tiles[:, tile_cols : 2 * tile_cols]])
    trace_parts = jnp.sum(factor_tiles * diag_tile[None], axis=(1, 2))
    square_parts = jnp.sum(factor_tiles * factor_tiles, axis=(1, 2))
    trace_sums, square_sums = (over_axes(trace_parts, DP_GRP), over_axes(square_parts, DP_GRP))
    damp_terms = damping * trace_sums / D
    norm_square = square_sums + 2.0 * damp_terms * trace_sums + D * damp_terms * damp_terms
    scale_factors = lax.rsqrt(norm_square)[:, None, None]
    base_tiles = (
        scale_factors * (factor_tiles + damp_terms[:, None, None] * diag_tile[None])
    ).astype(jnp.bfloat16)
    base_rows = row_panel(base_tiles)
    iterate_tiles = (2.0 * diag_tile[None] - base_tiles.astype(jnp.float32)).astype(jnp.bfloat16)
    iterate_rows = (2.0 * diag_rows[None] - base_rows.astype(jnp.float32)).astype(jnp.bfloat16)
    for sweep_index in range(ITERS - 1):
        product = times_columns(base_rows, iterate_tiles)
        product_tiles = product.astype(jnp.bfloat16)
        updated = 2.0 * iterate_tiles.astype(jnp.float32) - times_columns(
            iterate_rows, product_tiles
        )
        iterate_tiles = updated.astype(jnp.bfloat16)
        if sweep_index + 2 < ITERS:
            iterate_rows = row_panel(iterate_tiles)
    inverse_rows = row_panel(iterate_tiles[1:2])
    left_side = times_columns(inverse_rows, gradient_tile.astype(jnp.bfloat16)[None])
    left_tiles = left_side.astype(jnp.bfloat16)
    left_rows = row_panel(left_tiles)
    preconditioned = times_columns(left_rows, iterate_tiles[0:1])[0]
    square_total = over_axes(jnp.sum(preconditioned * preconditioned), DP_GRP)
    return preconditioned * lax.rsqrt(square_total / (D * D) + epsilon)


def solution(mesh):
    split = Mesh(mesh.devices.reshape(8, 2, 2, 2, 4), ("dp_0", "dp_1", "dp_2", "grp_0", "grp_1"))
    return jax.shard_map(
        shards, mesh=split, in_specs=(P(DP, GRP), P(DP, GRP)), out_specs=P(DP, GRP), check_vma=False
    )
```

profile of v0, /device:TPU:16, one launch (start us, length us, event | category | flops | bytes accessed | tf_op | source)
XLA Modules:
  0.0 806.2 jit_solution(5513607981691237652)
XLA Ops:
  6.5 2.1 pad_maximum_fusion.1
  8.7 104.8 %all-gather.9.cloned.1.call-done = bf16[1024,3072]{1,0:T(8,128)(2,1)} async-done(((bf16[1024,384]{1,0:T(8,128)(2,1)}), bf16[1024,3072]{1,0:T(8,128)(2,1)}) %all-gather.9.cloned.1.call-update) | async-done | bytes 6291472 | tf_op jit(solution)/shard_map/all_gather | solution.py:34
  113.5 3.6 fusion
  117.1 0.2 copy-done
  117.3 1.5 fusion.2
  118.8 1.5 fusion.4
  120.3 5.7 pad_maximum_fusion
  126.0 15.2 %copy.6 = f32[3072,1152]{1,0:T(8,128)} copy(f32[3072,1152]{0,1:T(8,128)} %pad_maximum_fusion) | data formatting | bytes 28311552 | tf_op jit(solution)/shard_map/concatenate | solution.py:104
  141.2 11.4 %copy.7 = f32[2,8,2,96,1152]{4,3,2,1,0:T(8,128)} copy(f32[2,8,2,96,1152]{4,3,0,2,1:T(8,128)} %bitcast.48) | data formatting | bytes 28311552 | tf_op jit(solution)/shard_map/transpose | solution.py:44
  152.6 31.1 %reduce-scatter.4.cloned.1.call-done = f32[16,96,1152]{2,1,0:T(8,128)} async-done(((f32[32,96,1152]{2,1,0:T(8,128)}), f32[16,96,1152]{2,1,0:T(8,128)}) %reduce-scatter.4.cloned.1.call-update) | async-done | bytes 7077904 | tf_op jit(solution)/shard_map/reduce_scatter | solution.py:46
  183.8 86.4 %reduce-scatter.6.cloned.1.call-done = f32[2,96,1152]{2,1,0:T(8,128)} async-done(((f32[16,96,1152]{2,1,0:T(8,128)}), f32[2,96,1152]{2,1,0:T(8,128)}) %reduce-scatter.6.cloned.1.call-update) | async-done | bytes 884752 | tf_op jit(solution)/shard_map/reduce_scatter | solution.py:46
  270.4 24.2 %reduce-scatter.8.cloned.1.call-done = f32[1,96,1152]{2,1,0:T(8,128)} async-done(((f32[2,96,1152]{2,1,0:T(8,128)}), f32[1,96,1152]{2,1,0:T(8,128)}) %reduce-scatter.8.cloned.1.call-update) | async-done | bytes 442384 | tf_op jit(solution)/shard_map/reduce_scatter | solution.py:46
  294.6 1.0 slice_bitcast_fusion.1
  295.6 0.2 multiply_reduce_fusion.1
  295.8 17.5 %all-reduce = (f32[2]{0:T(128)S(1)}, f32[2]{0:T(128)S(1)}) all-reduce(f32[2]{0:T(128)S(1)} %get-tuple-element.6, f32[2]{0:T(128)S(1)} %get-tuple-element.5), channel_id=1, replica_groups=mesh['dp_0'=8,'dp_1'=2,'dp_2'=2,'grp_0'=2,'grp_1'=4] {'dp_0'}, use_global_device_ids=true, to_apply=%region_10.0 | all-reduce | flops 4 | bytes 32 | tf_op jit(solution)/shard_map/psum | solution.py:62
  313.2 4.9 all-reduce.4
  318.1 2.4 all-reduce.3
  320.6 6.4 all-reduce.2
  327.0 10.4 %all-reduce.1 = (f32[2]{0:T(128)S(1)}, f32[2]{0:T(128)S(1)}) all-reduce(f32[2]{0:T(128)S(1)} %get-tuple-element.11, f32[2]{0:T(128)S(1)} %get-tuple-element.12), channel_id=1, replica_groups=mesh['dp_0'=8,'dp_1'=2,'dp_2'=2,'grp_0'=2,'grp_1'=4] {'grp_1'}, use_global_device_ids=true, to_apply=%region_14.0 | all-reduce | flops 4 | bytes 32 | tf_op jit(solution)/shard_map/psum | solution.py:62
  337.4 0.8 subtract_convert_fusion.6
  338.2 0.1 broadcast_in_dim.10
  338.4 17.9 %all_to_all.20 = bf16[8,2,96,384]{3,2,1,0:T(8,128)(2,1)S(1)} all-to-all(bf16[8,2,96,384]{3,2,1,0:T(8,128)(2,1)S(1)} %broadcast_in_dim.10), channel_id=1, replica_groups=mesh['dp_0'=8,'dp_1'=2,'dp_2'=2,'grp_0'=2,'grp_1'=4] {'grp_0','grp_1'}, dimensions={0} | all-to-all | bytes 2359296 | tf_op jit(solution)/shard_map/all_to_all | solution.py:18
  356.3 0.2 copy.12
  356.5 47.5 %all-gather.11.cloned.1.call-done = bf16[2,3072,384]{2,1,0:T(8,128)(2,1)} async-done(((bf16[2,96,384]{2,1,0:T(8,128)(2,1)}), bf16[2,3072,384]{2,1,0:T(8,128)(2,1)}) %all-gather.11.cloned.1.call-update) | async-done | bytes 4718608 | tf_op jit(solution)/shard_map/all_gather | solution.py:74
  404.0 4.0 convolution_convert_fusion.1
  408.0 0.2 fusion.10
  408.2 65.1 %all-gather.13.cloned.1.call-done = bf16[2,3072,384]{2,1,0:T(8,128)(2,1)} async-done(((bf16[2,96,384]{2,1,0:T(8,128)(2,1)}), bf16[2,3072,384]{2,1,0:T(8,128)(2,1)}) %all-gather.13.cloned.1.call-update) | async-done | bytes 4718608 | tf_op jit(solution)/shard_map/all_gather | solution.py:74
  473.2 4.0 fusion.12
  477.3 67.0 %all-gather.15.cloned.1.call-done = bf16[2,3072,384]{2,1,0:T(8,128)(2,1)} async-done(((bf16[2,96,384]{2,1,0:T(8,128)(2,1)}), bf16[2,3072,384]{2,1,0:T(8,128)(2,1)}) %all-gather.15.cloned.1.call-update) | async-done | bytes 4718608 | tf_op jit(solution)/shard_map/all_gather | solution.py:74
  544.3 3.9 convolution_convert_fusion
  548.3 1.5 slice.49
  550.1 23.0 %all_to_all.21 = bf16[8,2,96,384]{3,2,1,0:T(8,128)(2,1)S(1)} all-to-all(bf16[8,2,96,384]{3,2,1,0:T(8,128)(2,1)S(1)} %broadcast_in_dim.11), channel_id=1, replica_groups=mesh['dp_0'=8,'dp_1'=2,'dp_2'=2,'grp_0'=2,'grp_1'=4] {'grp_0','grp_1'}, dimensions={0} | all-to-all | bytes 2359296 | tf_op jit(solution)/shard_map/all_to_all | solution.py:18
  573.1 0.2 copy.13
  573.3 46.7 %all-gather.17.cloned.1.call-done = bf16[2,3072,384]{2,1,0:T(8,128)(2,1)} async-done(((bf16[2,96,384]{2,1,0:T(8,128)(2,1)}), bf16[2,3072,384]{2,1,0:T(8,128)(2,1)}) %all-gather.17.cloned.1.call-update) | async-done | bytes 4718608 | tf_op jit(solution)/shard_map/all_gather | solution.py:74
  620.1 3.3 fusion.13
  623.3 0.7 fusion.17
  624.1 17.1 %all_to_all.22 = bf16[8,1,96,384]{3,2,1,0:T(8,128)(2,1)S(1)} all-to-all(bf16[8,1,96,384]{3,2,1,0:T(8,128)(2,1)S(1)} %broadcast_in_dim.12), channel_id=1, replica_groups=mesh['dp_0'=8,'dp_1'=2,'dp_2'=2,'grp_0'=2,'grp_1'=4] {'grp_0','grp_1'}, dimensions={0} | all-to-all | bytes 1179648 | tf_op jit(solution)/shard_map/all_to_all | solution.py:18
  641.2 44.7 %all-gather.21.cloned.1.call-done = bf16[3072,384]{1,0:T(8,128)(2,1)} async-done(((bf16[96,384]{1,0:T(8,128)(2,1)}), bf16[3072,384]{1,0:T(8,128)(2,1)}) %all-gather.21.cloned.1.call-update) | async-done | bytes 2359312 | tf_op jit(solution)/shard_map/all_gather | solution.py:74
  685.9 2.2 convolution_convert_fusion.2
  688.2 16.8 %all_to_all.23 = bf16[8,1,96,384]{3,2,1,0:T(8,128)(2,1)S(1)} all-to-all(bf16[8,1,96,384]{3,2,1,0:T(8,128)(2,1)S(1)} %broadcast_in_dim.28), channel_id=1, replica_groups=mesh['dp_0'=8,'dp_1'=2,'dp_2'=2,'grp_0'=2,'grp_1'=4] {'grp_0','grp_1'}, dimensions={0} | all-to-all | bytes 1179648 | tf_op jit(solution)/shard_map/all_to_all | solution.py:18
  705.0 46.9 %all-gather.19.cloned.1.call-done = bf16[1,3072,384]{2,1,0:T(8,128)(2,1)} async-done(((bf16[1,96,384]{2,1,0:T(8,128)(2,1)}), bf16[1,3072,384]{2,1,0:T(8,128)(2,1)}) %all-gather.19.cloned.1.call-update) | async-done | bytes 2359312 | tf_op jit(solution)/shard_map/all_gather | solution.py:74
  751.9 2.8 multiply_reduce_fusion.2
  754.7 16.6 %psum.115 = f32[]{:T(128)} all-reduce(f32[]{:T(128)} %get-tuple-element.25), channel_id=1, replica_groups=mesh['dp_0'=8,'dp_1'=2,'dp_2'=2,'grp_0'=2,'grp_1'=4] {'dp_0'}, use_global_device_ids=true, to_apply=%region_16.0 | all-reduce | flops 1 | bytes 8 | tf_op jit(solution)/shard_map/psum | solution.py:62
  771.3 5.5 psum.116
  776.8 3.1 psum.117
  779.9 7.1 psum.118
  787.0 11.1 %psum.119 = f32[]{:T(128)} all-reduce(f32[]{:T(128)} %psum.118), channel_id=1, replica_groups=mesh['dp_0'=8,'dp_1'=2,'dp_2'=2,'grp_0'=2,'grp_1'=4] {'grp_1'}, use_global_device_ids=true, to_apply=%region_20.0 | all-reduce | flops 1 | bytes 8 | tf_op jit(solution)/shard_map/psum | solution.py:62
  798.7 0.7 broadcast_multiply_fusion
  (39 shorter events, 1.1 us)
Async XLA Ops:
  6.5 106.9 %all-gather.9.cloned.1.call-start = ((), (), s32[]{:S(2)}) async-start(), calls=%async_computation.7 | async-start | bytes 7077888 | tf_op jit(solution)/shard_map/all_gather | solution.py:34
  8.6 108.4 %copy-start.2 = (bf16[512,384]{1,0:T(8,128)(2,1)S(1)}, bf16[512,384]{1,0:T(8,128)(2,1)}, u32[]{:S(2)}) copy-start(bf16[512,384]{1,0:T(8,128)(2,1)} %param.2) | copy-start | bytes 1179652
  8.7 175.1 %reduce-scatter.4.cloned.1.call-start = ((), (), s32[]{:S(2)}) async-start(), calls=%async_computation.8 | async-start | bytes 21233664 | tf_op jit(solution)/shard_map/reduce_scatter | solution.py:46
  113.5 3.8 copy-start
  117.3 1.5 copy-start.3
  152.6 117.6 %reduce-scatter.6.cloned.1.call-start = ((), (), s32[]{:S(2)}) async-start(), calls=%async_computation.9 | async-start | bytes 7962624 | tf_op jit(solution)/shard_map/reduce_scatter | solution.py:46
  183.7 110.8 %reduce-scatter.8.cloned.1.call-start = ((), (), s32[]{:S(2)}) async-start(), calls=%async_computation.10 | async-start | bytes 1327104 | tf_op jit(solution)/shard_map/reduce_scatter | solution.py:46
  270.2 133.8 %all-gather.11.cloned.1.call-start = ((), (), s32[]{:S(2)}) async-start(), calls=%async_computation.11 | async-start | bytes 4866048 | tf_op jit(solution)/shard_map/all_gather | solution.py:74
  338.2 135.1 %all-gather.13.cloned.1.call-start = ((), (), s32[]{:S(2)}) async-start(), calls=%async_computation.12 | async-start | bytes 4866048 | tf_op jit(solution)/shard_map/all_gather | solution.py:74
  404.0 69.3 %copy-start.4 = (bf16[2,96,384]{2,1,0:T(8,128)(2,1)S(1)}, bf16[2,96,384]{2,1,0:T(8,128)(2,1)}, u32[]{:S(2)}) copy-start(bf16[2,96,384]{2,1,0:T(8,128)(2,1)} %get-tuple-element.17) | copy-start | bytes 442372
  407.9 136.4 %all-gather.15.cloned.1.call-start = ((), (), s32[]{:S(2)}) async-start(), calls=%async_computation.13 | async-start | bytes 4866048 | tf_op jit(solution)/shard_map/all_gather | solution.py:74
  477.2 72.7 %copy-start.1 = (bf16[2,96,384]{2,1,0:T(8,128)(2,1)S(1)}, bf16[2,96,384]{2,1,0:T(8,128)(2,1)}, u32[]{:S(2)}) copy-start(bf16[2,96,384]{2,1,0:T(8,128)(2,1)} %fusion.12) | copy-start | bytes 442372
  477.2 142.8 %all-gather.17.cloned.1.call-start = ((), (), s32[]{:S(2)}) async-start(), calls=%async_computation.14 | async-start | bytes 4866048 | tf_op jit(solution)/shard_map/all_gather | solution.py:74
  548.3 137.7 %all-gather.21.cloned.1.call-start = ((), (), s32[]{:S(2)}) async-start(), calls=%async_computation.16 | async-start | bytes 2433024 | tf_op jit(solution)/shard_map/all_gather | solution.py:74
  549.9 202.0 %all-gather.19.cloned.1.call-start = ((), (), s32[]{:S(2)}) async-start(), calls=%async_computation.15 | async-start | bytes 2433024 | tf_op jit(solution)/shard_map/all_gather | solution.py:74
Sparse Core Ops, SparseCore 0:
  9.8 103.6 all-gather.8
  152.7 30.9 reduce-scatter.3
  186.3 83.8 reduce-scatter.5
  272.5 22.0 reduce-scatter.7
  338.3 65.5 all-gather.10
  408.1 65.1 all-gather.12
  477.3 66.9 all-gather.14
  548.4 71.6 all-gather.16
  621.9 63.9 all-gather.20
  687.6 64.2 all-gather.18
where the time goes:
time: 807 us; the launch traced here: 806 us
  waiting for transfers between devices  564 us (70%)
  blocking collectives  160 us (20%)
  local copies, waits for them, and re-layouts  30.9 us (4%)
  matrix products  26.7 us (3%)
  between operations  14.4 us (2%)
  other arithmetic  9.71 us (1%)
    all_gather x6, waiting for transfers between devices, times_columns(): lax.all_gather(stacked_tiles, DP, axis=1, tiled=True)  318 us
    reduce_scatter x3, waiting for transfers between devices, own_block(): tiles = lax.psum_scatter(tiles, axes[k], scatter_dimension=0, tiled=True)  142 us
    all_gather x1, waiting for transfers between devices, sent_together(): whole, at, outs = (lax.all_gather(both, axis, axis=dim, tiled=True), 0, [])  105 us
    psum x10, blocking collectives, over_axes(): shard = lax.psum(shard, axis)  84.9 us
    all_to_all x4, blocking collectives, copy_for_each(): return lax.all_to_all(copies, axis, split_axis=0, concat_axis=0, tiled=True)  74.8 us
    dot_general x6, matrix products, times_columns(): jnp.einsum('fri,fic->frc', panel_rows, lax.all_gather(stacked_tiles, DP,...  20.1 us
  transfers between devices with their start and end apart: 10, of which 10 were waited for; matrix products, arithmetic and copies ran while one was open for 1% of the time, Pallas kernels for 0%

commit v1 on v0

--- a/solution.py
+++ b/solution.py
@@ -71,7 +71,9 @@
     return jnp.einsum(
         "fri,fic->frc",
         panel_rows,
-        lax.all_gather(stacked_tiles, DP, axis=1, tiled=True),
+        jnp.concatenate(
+            lax.all_to_all(jnp.stack([stacked_tiles] * lax.axis_size(DP)), DP, 0, 0), axis=1
+        ),
         preferred_element_type=jnp.float32,
     )
 

time: 807 us -> 1060 us (1.31)
  waiting for transfers between devices: 564 us -> 694 us
  blocking collectives: 160 us -> 230 us
  starting transfers between devices: 0.37 us -> 39.8 us
  local copies, waits for them, and re-layouts: 30.9 us -> 56.9 us
  matrix products: 26.7 us -> 12.3 us
    all_to_all x0 -> x7, waiting for transfers between devices: none -> 447 us  [the longest x5 429 us: times_columns(): lax.all_to_all(jnp.stack([stacked_tiles] * lax.axis_size(DP)), DP, 0, 0)]
    all_gather x6 -> x0, waiting for transfers between devices: 318 us -> none  [times_columns(): lax.all_gather(stacked_tiles, DP, axis=1, tiled=True)]
    all_to_all x0 -> x1, blocking collectives: none -> 113 us  [times_columns(): lax.all_to_all(jnp.stack([stacked_tiles] * lax.axis_size(DP)), DP, 0, 0)]
    all_to_all x4 -> x2, blocking collectives: 74.8 us -> 32.8 us  [copy_for_each(): return lax.all_to_all(copies, axis, split_axis=0, concat_axis=0, tiled=True)]
    all_to_all x0 -> x7, starting transfers between devices: none -> 39.6 us  [the longest x5 27 us: times_columns(): lax.all_to_all(jnp.stack([stacked_tiles] * lax.axis_size(DP)), DP, 0, 0)]
    dot_general x6, matrix products: 20.1 us -> 5.68 us  [times_columns(): jnp.einsum('fri,fic->frc', panel_rows, jnp.concatenate(lax.all_to_all(jnp...]
    another operation x0 -> x6, local copies, waits for them, and re-layouts: none -> 13.5 us  [times_columns(): jnp.stack([stacked_tiles] * lax.axis_size(DP))]
    reshape x0 -> x4, local copies, waits for them, and re-layouts: none -> 11.2 us  [times_columns(): jnp.concatenate(lax.all_to_all(jnp.stack([stacked_tiles] * lax.axis_size(...]
  transfers between devices with their start and end apart: 10 -> 11, of which waited for: 10 -> 11; matrix products, arithmetic and copies ran while one was open for 1% -> 1% of each run, Pallas kernels for 0% -> 0%
where the time goes in v1:
time: 1060 us
  waiting for transfers between devices  694 us (65%)
  blocking collectives  230 us (22%)
  local copies, waits for them, and re-layouts  56.9 us (5%)
  starting transfers between devices  39.8 us (4%)
  between operations  14.1 us (1%)
  matrix products  12.3 us (1%)
    all_to_all x5, waiting for transfers between devices, times_columns(): lax.all_to_all(jnp.stack([stacked_tiles] * lax.axis_size(DP)), DP, 0, 0)  429 us
    reduce_scatter x3, waiting for transfers between devices, own_block(): tiles = lax.psum_scatter(tiles, axes[k], scatter_dimension=0, tiled=True)  142 us
    all_to_all x1, blocking collectives, times_columns(): lax.all_to_all(jnp.stack([stacked_tiles] * lax.axis_size(DP)), DP, 0, 0)  113 us
    all_gather x1, waiting for transfers between devices, sent_together(): whole, at, outs = (lax.all_gather(both, axis, axis=dim, tiled=True), 0, [])  105 us
    psum x10, blocking collectives, over_axes(): shard = lax.psum(shard, axis)  83.9 us
    all_to_all x2, blocking collectives, copy_for_each(): return lax.all_to_all(copies, axis, split_axis=0, concat_axis=0, tiled=True)  32.8 us
    all_to_all x5, starting transfers between devices, times_columns(): lax.all_to_all(jnp.stack([stacked_tiles] * lax.axis_size(DP)), DP, 0, 0)  27 us
  transfers between devices with their start and end apart: 11, of which 11 were waited for; matrix products, arithmetic and copies ran while one was open for 1% of the time, Pallas kernels for 0%

profile of v1, /device:TPU:16, one launch (start us, length us, event | category | flops | bytes accessed | tf_op | source)
XLA Modules:
  0.0 1055.9 jit_solution(13868586909384710988)
XLA Ops:
  6.5 2.1 pad_maximum_fusion.1
  8.7 104.8 %all-gather.2.cloned.1.call-done = bf16[1024,3072]{1,0:T(8,128)(2,1)} async-done(((bf16[1024,384]{1,0:T(8,128)(2,1)}), bf16[1024,3072]{1,0:T(8,128)(2,1)}) %all-gather.2.cloned.1.call-update) | async-done | bytes 6291472 | tf_op jit(solution)/shard_map/all_gather | solution.py:34
  113.5 3.6 fusion
  117.3 1.5 fusion.2
  118.8 1.5 fusion.4
  120.3 5.7 pad_maximum_fusion
  126.0 15.2 %copy.6 = f32[3072,1152]{1,0:T(8,128)} copy(f32[3072,1152]{0,1:T(8,128)} %pad_maximum_fusion) | data formatting | bytes 28311552 | tf_op jit(solution)/shard_map/concatenate | solution.py:106
  141.2 11.4 %copy.7 = f32[2,8,2,96,1152]{4,3,2,1,0:T(8,128)} copy(f32[2,8,2,96,1152]{4,3,0,2,1:T(8,128)} %bitcast.56) | data formatting | bytes 28311552 | tf_op jit(solution)/shard_map/transpose | solution.py:44
  152.6 31.1 %reduce-scatter.4.cloned.1.call-done = f32[16,96,1152]{2,1,0:T(8,128)} async-done(((f32[32,96,1152]{2,1,0:T(8,128)}), f32[16,96,1152]{2,1,0:T(8,128)}) %reduce-scatter.4.cloned.1.call-update) | async-done | bytes 7077904 | tf_op jit(solution)/shard_map/reduce_scatter | solution.py:46
  183.8 86.4 %reduce-scatter.6.cloned.1.call-done = f32[2,96,1152]{2,1,0:T(8,128)} async-done(((f32[16,96,1152]{2,1,0:T(8,128)}), f32[2,96,1152]{2,1,0:T(8,128)}) %reduce-scatter.6.cloned.1.call-update) | async-done | bytes 884752 | tf_op jit(solution)/shard_map/reduce_scatter | solution.py:46
  270.4 24.2 %reduce-scatter.8.cloned.1.call-done = f32[1,96,1152]{2,1,0:T(8,128)} async-done(((f32[2,96,1152]{2,1,0:T(8,128)}), f32[1,96,1152]{2,1,0:T(8,128)}) %reduce-scatter.8.cloned.1.call-update) | async-done | bytes 442384 | tf_op jit(solution)/shard_map/reduce_scatter | solution.py:46
  295.7 17.5 %all-reduce = (f32[2]{0:T(128)S(1)}, f32[2]{0:T(128)S(1)}) all-reduce(f32[2]{0:T(128)S(1)} %get-tuple-element.6, f32[2]{0:T(128)S(1)} %get-tuple-element.5), channel_id=1, replica_groups=mesh['dp_0'=8,'dp_1'=2,'dp_2'=2,'grp_0'=2,'grp_1'=4] {'dp_0'}, use_global_device_ids=true, to_apply=%region_10.0 | all-reduce | flops 4 | bytes 32 | tf_op jit(solution)/shard_map/psum | solution.py:62
  313.2 4.9 all-reduce.4
  318.1 2.4 all-reduce.3
  320.6 6.4 all-reduce.2
  327.0 10.4 all-reduce.1
  337.6 17.7 %all_to_all.50 = bf16[8,2,96,384]{3,2,1,0:T(8,128)(2,1)S(1)} all-to-all(bf16[8,2,96,384]{3,2,1,0:T(8,128)(2,1)S(1)} %broadcast_in_dim.8), channel_id=1, replica_groups=mesh['dp_0'=8,'dp_1'=2,'dp_2'=2,'grp_0'=2,'grp_1'=4] {'grp_0','grp_1'}, dimensions={0} | all-to-all | bytes 2359296 | tf_op jit(solution)/shard_map/all_to_all | solution.py:18
  355.3 2.9 stack.21
  358.2 5.1 all-to-all-start.1
  363.6 105.2 %all-to-all-done.1 = bf16[32,2,96,384]{3,2,1,0:T(8,128)(2,1)} async-done(((bf16[32,2,96,384]{3,2,1,0:T(8,128)(2,1)}), bf16[32,2,96,384]{3,2,1,0:T(8,128)(2,1)}, u32[]{:S(2)}, u32[]{:S(2)}) %all-to-all-start.1) | async-done | bytes 4718624 | tf_op jit(solution)/shard_map/all_to_all | solution.py:75
  468.7 2.8 copy.9
  472.5 2.9 stack.22
  475.4 6.1 all-to-all-start.2
  481.7 104.9 %all-to-all-done.2 = bf16[32,2,96,384]{3,2,1,0:T(8,128)(2,1)} async-done(((bf16[32,2,96,384]{3,2,1,0:T(8,128)(2,1)}), bf16[32,2,96,384]{3,2,1,0:T(8,128)(2,1)}, u32[]{:S(2)}, u32[]{:S(2)}) %all-to-all-start.2) | async-done | bytes 4718624 | tf_op jit(solution)/shard_map/all_to_all | solution.py:75
  586.6 2.8 copy.10
  591.2 113.2 %all_to_all.51 = bf16[32,2,96,384]{3,2,1,0:T(8,128)(2,1)} all-to-all(bf16[32,2,96,384]{3,2,1,0:T(8,128)(2,1)S(1)} %stack.23), channel_id=1, replica_groups=mesh['dp_0'=8,'dp_1'=2,'dp_2'=2,'grp_0'=2,'grp_1'=4] {'dp_0','dp_1','dp_2'}, dimensions={0} | all-to-all | bytes 9437184 | tf_op jit(solution)/shard_map/all_to_all | solution.py:75
  704.4 1.2 broadcast_in_dim.9
  705.6 6.2 all-to-all-start.3
  711.8 2.8 copy.12
  715.6 11.7 %all-to-all-done.3 = bf16[8,2,96,384]{3,2,1,0:T(8,128)(2,1)S(1)} async-done(((bf16[8,2,96,384]{3,2,1,0:T(8,128)(2,1)}), bf16[8,2,96,384]{3,2,1,0:T(8,128)(2,1)S(1)}, u32[]{:S(2)}, u32[]{:S(2)}) %all-to-all-start.3) | async-done | bytes 1179680 | tf_op jit(solution)/shard_map/all_to_all | solution.py:18
  727.3 2.9 stack.24
  730.2 4.9 all-to-all-start.5
  735.3 107.6 %all-to-all-done.5 = bf16[32,2,96,384]{3,2,1,0:T(8,128)(2,1)} async-done(((bf16[32,2,96,384]{3,2,1,0:T(8,128)(2,1)}), bf16[32,2,96,384]{3,2,1,0:T(8,128)(2,1)}, u32[]{:S(2)}, u32[]{:S(2)}) %all-to-all-start.5) | async-done | bytes 4718624 | tf_op jit(solution)/shard_map/all_to_all | solution.py:75
  842.9 2.8 copy.13
  848.2 6.5 all-to-all-start.6
  855.6 6.6 all-to-all-done.6
  862.2 1.6 stack.25
  863.9 6.1 all-to-all-start.7
  870.0 55.7 %all-to-all-done.7 = bf16[32,1,96,384]{3,2,1,0:T(8,128)(2,1)S(1)} async-done(((bf16[32,1,96,384]{3,2,1,0:T(8,128)(2,1)}), bf16[32,1,96,384]{3,2,1,0:T(8,128)(2,1)S(1)}, u32[]{:S(2)}, u32[]{:S(2)}) %all-to-all-start.7) | async-done | bytes 2359328 | tf_op jit(solution)/shard_map/all_to_all | solution.py:75
  926.3 15.1 %all_to_all.52 = bf16[8,1,96,384]{3,2,1,0:T(8,128)(2,1)S(1)} all-to-all(bf16[8,1,96,384]{3,2,1,0:T(8,128)(2,1)S(1)} %broadcast_in_dim.11), channel_id=1, replica_groups=mesh['dp_0'=8,'dp_1'=2,'dp_2'=2,'grp_0'=2,'grp_1'=4] {'grp_0','grp_1'}, dimensions={0} | all-to-all | bytes 1179648 | tf_op jit(solution)/shard_map/all_to_all | solution.py:18
  941.4 2.5 stack.26
  943.9 4.9 all-to-all-start.9
  948.9 55.7 %all-to-all-done.9 = bf16[32,1,96,384]{3,2,1,0:T(8,128)(2,1)S(1)} async-done(((bf16[32,1,96,384]{3,2,1,0:T(8,128)(2,1)}), bf16[32,1,96,384]{3,2,1,0:T(8,128)(2,1)S(1)}, u32[]{:S(2)}, u32[]{:S(2)}) %all-to-all-start.9) | async-done | bytes 2359328 | tf_op jit(solution)/shard_map/all_to_all | solution.py:75
  1005.7 16.9 %psum.115 = f32[]{:T(128)} all-reduce(f32[]{:T(128)} %get-tuple-element.25), channel_id=1, replica_groups=mesh['dp_0'=8,'dp_1'=2,'dp_2'=2,'grp_0'=2,'grp_1'=4] {'dp_0'}, use_global_device_ids=true, to_apply=%region_16.0 | all-reduce | flops 1 | bytes 8 | tf_op jit(solution)/shard_map/psum | solution.py:62
  1022.7 5.5 psum.116
  1028.2 3.1 psum.117
  1031.3 7.1 psum.118
  1038.3 9.7 psum.119
  (40 shorter events, 12.3 us)
Async XLA Ops:
  6.5 106.9 %all-gather.2.cloned.1.call-start = ((), (), s32[]{:S(2)}) async-start(), calls=%async_computation.13 | async-start | bytes 7077888 | tf_op jit(solution)/shard_map/all_gather | solution.py:34
  8.6 108.4 %copy-start.1 = (bf16[512,384]{1,0:T(8,128)(2,1)S(1)}, bf16[512,384]{1,0:T(8,128)(2,1)}, u32[]{:S(2)}) copy-start(bf16[512,384]{1,0:T(8,128)(2,1)} %param.2) | copy-start | bytes 1179652
  8.7 175.1 %reduce-scatter.4.cloned.1.call-start = ((), (), s32[]{:S(2)}) async-start(), calls=%async_computation.14 | async-start | bytes 21233664 | tf_op jit(solution)/shard_map/reduce_scatter | solution.py:46
  113.5 3.8 copy-start
  117.3 1.5 copy-start.2
  152.6 117.6 %reduce-scatter.6.cloned.1.call-start = ((), (), s32[]{:S(2)}) async-start(), calls=%async_computation.15 | async-start | bytes 7962624 | tf_op jit(solution)/shard_map/reduce_scatter | solution.py:46
  183.7 110.8 %reduce-scatter.8.cloned.1.call-start = ((), (), s32[]{:S(2)}) async-start(), calls=%async_computation.16 | async-start | bytes 1327104 | tf_op jit(solution)/shard_map/reduce_scatter | solution.py:46
  358.2 110.5 %all-to-all-start.1 = ((bf16[32,2,96,384]{3,2,1,0:T(8,128)(2,1)}), bf16[32,2,96,384]{3,2,1,0:T(8,128)(2,1)}, u32[]{:S(2)}, u32[]{:S(2)}) async-start(bf16[32,2,96,384]{3,2,1,0:T(8,128)(2,1)} %stack.21), calls=%async_computation.4 | async-start | bytes 9437184 | tf_op jit(solution)/shard_map/all_to_all | solution.py:75
  475.4 111.2 %all-to-all-start.2 = ((bf16[32,2,96,384]{3,2,1,0:T(8,128)(2,1)}), bf16[32,2,96,384]{3,2,1,0:T(8,128)(2,1)}, u32[]{:S(2)}, u32[]{:S(2)}) async-start(bf16[32,2,96,384]{3,2,1,0:T(8,128)(2,1)} %stack.22), calls=%async_computation.5 | async-start | bytes 9437184 | tf_op jit(solution)/shard_map/all_to_all | solution.py:75
  705.6 21.7 %all-to-all-start.3 = ((bf16[8,2,96,384]{3,2,1,0:T(8,128)(2,1)}), bf16[8,2,96,384]{3,2,1,0:T(8,128)(2,1)S(1)}, u32[]{:S(2)}, u32[]{:S(2)}) async-start(bf16[8,2,96,384]{3,2,1,0:T(8,128)(2,1)} %broadcast_in_dim.9), calls=%async_computation.6 | async-start | bytes 2359296 | tf_op jit(solution)/shard_map/all_to_all | solution.py:18
  730.2 112.7 %all-to-all-start.5 = ((bf16[32,2,96,384]{3,2,1,0:T(8,128)(2,1)}), bf16[32,2,96,384]{3,2,1,0:T(8,128)(2,1)}, u32[]{:S(2)}, u32[]{:S(2)}) async-start(bf16[32,2,96,384]{3,2,1,0:T(8,128)(2,1)} %stack.24), calls=%async_computation.8 | async-start | bytes 9437184 | tf_op jit(solution)/shard_map/all_to_all | solution.py:75
  848.2 14.0 %all-to-all-start.6 = ((bf16[8,1,96,384]{3,2,1,0:T(8,128)(2,1)}), bf16[8,1,96,384]{3,2,1,0:T(8,128)(2,1)S(1)}, u32[]{:S(2)}, u32[]{:S(2)}) async-start(bf16[8,1,96,384]{3,2,1,0:T(8,128)(2,1)} %broadcast_in_dim.10), calls=%async_computation.9 | async-start | bytes 1179648 | tf_op jit(solution)/shard_map/all_to_all | solution.py:18
  863.9 61.9 %all-to-all-start.7 = ((bf16[32,1,96,384]{3,2,1,0:T(8,128)(2,1)}), bf16[32,1,96,384]{3,2,1,0:T(8,128)(2,1)S(1)}, u32[]{:S(2)}, u32[]{:S(2)}) async-start(bf16[32,1,96,384]{3,2,1,0:T(8,128)(2,1)} %stack.25), calls=%async_computation.10 | async-start | bytes 4718592 | tf_op jit(solution)/shard_map/all_to_all | solution.py:75
  943.9 60.6 %all-to-all-start.9 = ((bf16[32,1,96,384]{3,2,1,0:T(8,128)(2,1)}), bf16[32,1,96,384]{3,2,1,0:T(8,128)(2,1)S(1)}, u32[]{:S(2)}, u32[]{:S(2)}) async-start(bf16[32,1,96,384]{3,2,1,0:T(8,128)(2,1)} %stack.26), calls=%async_computation.12 | async-start | bytes 4718592 | tf_op jit(solution)/shard_map/all_to_all | solution.py:75
Sparse Core Ops, SparseCore 0:
  9.8 103.6 all-gather.1
  152.7 30.9 reduce-scatter.3
  186.3 83.8 reduce-scatter.5
  272.5 22.0 reduce-scatter.7
